TPU v7x, 256 devices: a whole 4x4x8 slice. The times are simulated.
256 devices in a mesh: cg: 16 (over z, x_lo), vg: 16 (over x_hi, y, core).
Axes of the slice: x: 4 (x_hi: 2, x_lo: 2; x = x_hi * 2 + x_lo), y: 4, z: 8, core: 2. Of those that a mesh axis runs over, the one named last changes fastest.
Arguments:
- con_embed: float32 [262144, 128], P(('cg', 'vg')), may hold values from -6 to 6
- var_embed: float32 [262144, 128], P(('vg', 'cg')), may hold values from -6 to 6
- row_coef: float32 [262144], P(('cg', 'vg')), may hold values from 0.3 to 3
- col_coef: float32 [262144], P(('vg', 'cg')), may hold values from 0.3 to 3
- self_weight: float32 [128, 128], replicated, may hold values from -0.5 to 0.5
- msg_weight: float32 [128, 128], replicated, may hold values from -0.0234375 to 0.0234375
- timestep: int32 [1], replicated, may hold values from 0 to 999
- tile_rows: int32 [16, 16, 16], P('cg', 'vg'), may hold values from 0 to 31, as said below
- tile_cols: int32 [16, 16, 16], P('cg', 'vg'), may hold values from 0 to 31, as said below
- pattern: bfloat16 [16, 16, 16, 512, 512], P('cg', 'vg'), may hold values from -6 to 6
- cotangent: float32 [262144, 128], P(('cg', 'vg')), may hold values from -6 to 6
Outputs:
- con_update: float32 [262144, 128], P(('cg', 'vg'))
- grad_con: float32 [262144, 128], P(('cg', 'vg'))
- grad_var: float32 [262144, 128], P(('vg', 'cg'))
- grad_msg: float32 [128, 128], replicated
- grad_self: float32 [128, 128], replicated
Inputs may be any that keep to these rules, and one draw needn't show every extreme that they name: `tile_rows`: every device lists tile row 0 and tile row 31; a device lists distinct tiles unless 16 exceeds 32 * 32, and repeated tiles add. `tile_cols`: every device lists tile column 0 and tile column 31, together with the rows above: tiles (0, 0) and (31, 31) are on every list.
All inputs are finite; a program needn't handle non-finite values.
Results may differ from a plain program's by a relative error of at most 0.007.
Values may be sent and summed in bfloat16 or wider, within the bound.
No kernel may reach another device: no remote copies, remote signals or barrier semaphores. Data moves between devices by JAX's collectives and lax.ppermute only.
A program may use at most 128 MiB of HBM per device.

v0:
```python
import math
import jax
import jax.numpy as jnp
from jax import lax
from jax.sharding import PartitionSpec as P

H = 128
TB = 512


def body(
    con_embed,
    var_embed,
    row_coef,
    col_coef,
    self_weight,
    msg_weight,
    timestep,
    tile_rows,
    tile_cols,
    pattern,
    cotangent,
):
    highest = lax.Precision.HIGHEST
    con_count = con_embed.shape[0]
    var_count = var_embed.shape[0]
    row_blocks = con_count * lax.axis_size("vg") // TB
    col_blocks = var_count * lax.axis_size("cg") // TB
    row_index = tile_rows.reshape(-1)
    col_index = tile_cols.reshape(-1)
    tile_count = row_index.shape[0]
    per_turn = math.gcd(tile_count, 8)
    turns = tile_count // per_turn
    patterns_here = pattern.reshape(turns, per_turn, TB, TB)
    row_turns = row_index.reshape(turns, per_turn)
    col_turns = col_index.reshape(turns, per_turn)
    gathered, scales = (
        lax.all_gather(var_embed, "cg", axis=0, tiled=True),
        lax.all_gather(col_coef, "cg", axis=0, tiled=True),
    )
    projected = (
        jnp.dot(gathered, msg_weight, precision=highest, preferred_element_type=jnp.float32)
        * scales[:, None]
    ).astype(jnp.bfloat16)
    source_blocks = projected.reshape(col_blocks, TB, H)
    row_ids = jnp.arange(row_blocks, dtype=jnp.int32)
    col_ids = jnp.arange(col_blocks, dtype=jnp.int32)

    def forward_turn(running, inputs):
        rows_now, cols_now, tile_mask = inputs
        products = jnp.einsum(
            "grc,gch->grh", tile_mask, source_blocks[cols_now], preferred_element_type=jnp.float32
        )
        selector = (rows_now[None, :] == row_ids[:, None]).astype(jnp.float32)
        running = running + jnp.dot(
            selector,
            products.reshape(per_turn, TB * H),
            precision=highest,
            preferred_element_type=jnp.float32,
        )
        return (running, None)

    forward_sum, _ = lax.scan(
        forward_turn,
        jnp.zeros((row_blocks, TB * H), jnp.float32),
        (row_turns, col_turns, patterns_here),
    )
    messages = lax.psum_scatter(
        forward_sum.reshape(row_blocks * TB, H), "vg", scatter_dimension=0, tiled=True
    )
    frequency = jnp.exp(-math.log(10000.0) * jnp.arange(H // 2, dtype=jnp.float32) / (H // 2))
    phases = timestep[0].astype(jnp.float32) * frequency
    time_embed = jnp.concatenate([jnp.sin(phases), jnp.cos(phases)])
    preact = (
        jnp.dot(con_embed, self_weight, precision=highest, preferred_element_type=jnp.float32)
        + row_coef[:, None] * messages
        + time_embed[None, :]
    )
    sigmoid_z = jax.nn.sigmoid(preact)
    con_update = con_embed + preact * sigmoid_z
    grad_pre = cotangent * sigmoid_z * (1.0 + preact * (1.0 - sigmoid_z))
    grad_con = cotangent + jnp.dot(
        grad_pre, self_weight.T, precision=highest, preferred_element_type=jnp.float32
    )
    local_self = jnp.dot(
        con_embed.T, grad_pre, precision=highest, preferred_element_type=jnp.float32
    )
    grad_messages = (row_coef[:, None] * grad_pre).astype(jnp.bfloat16)
    whole_rows = lax.all_gather(grad_messages, "vg", axis=0, tiled=True).reshape(row_blocks, TB, H)

    def backward_turn(running, inputs):
        rows_now, cols_now, tile_mask = inputs
        products = jnp.einsum(
            "grc,grh->gch", tile_mask, whole_rows[rows_now], preferred_element_type=jnp.float32
        )
        selector = (cols_now[None, :] == col_ids[:, None]).astype(jnp.float32)
        running = running + jnp.dot(
            selector,
            products.reshape(per_turn, TB * H),
            precision=highest,
            preferred_element_type=jnp.float32,
        )
        return (running, None)

    backward_sum, _ = lax.scan(
        backward_turn,
        jnp.zeros((col_blocks, TB * H), jnp.float32),
        (row_turns, col_turns, patterns_here),
    )
    grad_projected = lax.psum_scatter(
        backward_sum.reshape(col_blocks * TB, H), "cg", scatter_dimension=0, tiled=True
    )
    grad_lin = col_coef[:, None] * grad_projected
    grad_var = jnp.dot(
        grad_lin, msg_weight.T, precision=highest, preferred_element_type=jnp.float32
    )
    local_msg = jnp.dot(
        var_embed.T, grad_lin, precision=highest, preferred_element_type=jnp.float32
    )
    grad_msg, grad_self = lax.psum((local_msg, local_self), ("cg", "vg"))
    return (con_update, grad_con, grad_var, grad_msg, grad_self)


def solution(mesh):
    in_specs = (
        P(("cg", "vg"), None),
        P(("vg", "cg"), None),
        P(("cg", "vg")),
        P(("vg", "cg")),
        P(),
        P(),
        P(),
        P("cg", "vg", None),
        P("cg", "vg", None),
        P("cg", "vg", None, None, None),
        P(("cg", "vg"), None),
    )
    out_specs = (P(("cg", "vg"), None), P(("cg", "vg"), None), P(("vg", "cg"), None), P(), P())
    return jax.shard_map(body, mesh=mesh, in_specs=in_specs, out_specs=out_specs, check_vma=False)
```

profile of v0, /device:TPU:2, one launch (start us, length us, event | category | flops | bytes accessed | tf_op | source)
XLA Modules:
  0.0 902.7 jit_solution(3706184754790364743)
XLA Ops:
  8.5 1.3 reduce.6
  11.3 37.0 %all_gather.10 = f32[16384]{0:T(1024)S(1)} all-gather(f32[1024]{0:T(1024)} %param.18), channel_id=1, replica_groups=mesh['cg'=16,'vg'=16] {'cg'}, dimensions={0}, use_global_device_ids=true | all-gather | bytes 69632 | tf_op jit(solution)/shard_map/all_gather | solution.py:39
  48.3 146.8 %all-gather.3.cloned.1.call-done = f32[16384,128]{1,0:T(8,128)} async-done(((f32[1024,128]{1,0:T(8,128)}), f32[16384,128]{1,0:T(8,128)}) %all-gather.3.cloned.1.call-update) | async-done | bytes 8388624 | tf_op jit(solution)/shard_map/all_gather | solution.py:38
  195.1 18.7 %fusion.30 = bf16[16384,128]{1,0:T(8,128)(2,1)} fusion(f32[16384,128]{1,0:T(8,128)} %all-gather.3.cloned.1.call-done, f32[128,128]{1,0:T(8,128)S(1)} %copy-done, f32[16384]{0:T(1024)S(1)} %all_gather.10), kind=kOutput, calls=%fused_computation.39 | convolution fusion | flops 3225419776 | bytes 12713984 | tf_op jit(solution)/shard_map/dot_general | solution.py:42
  213.8 30.1 %while.22 = (s32[]{:T(128)}, f32[32,65536]{1,0:T(8,128)}, s32[2,8]{1,0:T(2,128)S(1)}, bf16[2,8,512,512]{3,2,1,0:T(8,128)(2,1)}, s32[2,8]{1,0:T(2,128)S(1)}, /*in...) while((s32[]{:T(128)}, f32[32,65536]{1,0:T(8,128)}, s32[2,8]{1,0:T(2,128)S(1)}, ...), condition=%wide.region_1.2_spmd.clone, body=%wide.region_0.1_spmd.clone.sunk | while | flops 742393088 | bytes 28316484 | solution.py:63
  213.8 2.9 gather_fusion
  216.7 3.4 fusion.65
  220.2 7.5 convolution_add_fusion.6
  227.7 2.9 gather_fusion
  230.7 3.4 fusion.65
  234.1 9.7 %convolution_add_fusion.6 = f32[32,65536]{1,0:T(8,128)} fusion(f32[32,65536]{1,0:T(8,128)} %get-tuple-element.263, pred[]{:T(512)S(6)} %compare.6, f32[1,8,512,128]{3,2,1,0:T(8,128)S(1)} %fusion.65, s32[8]{0:T(128)S(1)} %fusion.66), kind=kOutput, calls=%fused_computation.4.clone.1 | convolution fusion | flops 205521152 | bytes 18874400 | tf_op jit(solution)/shard_map/while/body/eval_jaxpr/dot_general | solution.py:55
  243.8 7.3 reshape.96
  252.1 110.5 %reduce-scatter.3.cloned.1.call-done = f32[1024,128]{1,0:T(8,128)} async-done(((f32[16384,128]{1,0:T(8,128)}), f32[1024,128]{1,0:T(8,128)}) %reduce-scatter.3.cloned.1.call-update) | async-done | bytes 524304 | tf_op jit(solution)/shard_map/reduce_scatter | solution.py:68
  362.6 2.9 multiply_convert_fusion
  365.7 12.4 %copy.20 = bf16[1,1,16,512,512]{3,4,2,1,0:T(8,128)(2,1)} copy(bf16[1,1,16,512,512]{4,3,2,1,0:T(8,128)(2,1)} %bitcast.88) | data formatting | bytes 16777216 | tf_op args[9]
  378.0 47.1 %all-gather.5.cloned.1.call-done = bf16[16384,128]{1,0:T(8,128)(2,1)} async-done(((bf16[1024,128]{1,0:T(8,128)(2,1)}), bf16[16384,128]{1,0:T(8,128)(2,1)}) %all-gather.5.cloned.1.call-update) | async-done | bytes 4194320 | tf_op jit(solution)/shard_map/all_gather | solution.py:89
  425.2 29.9 %while.23 = (s32[]{:T(128)}, f32[32,65536]{1,0:T(8,128)}, s32[2,8]{1,0:T(2,128)S(1)}, bf16[2,8,512,512]{2,3,1,0:T(8,128)(2,1)}, s32[2,8]{1,0:T(2,128)S(1)}, /*in...) while((s32[]{:T(128)}, f32[32,65536]{1,0:T(8,128)}, s32[2,8]{1,0:T(2,128)S(1)}, ...), condition=%wide.region_4.5_spmd.clone, body=%wide.region_3.4_spmd.clone.sunk | while | flops 742393088 | bytes 28316484 | solution.py:105
  425.2 2.9 gather_fusion.1
  428.1 3.4 fusion.71
  431.6 7.4 convolution_add_fusion.7
  439.0 2.9 gather_fusion.1
  442.0 3.4 fusion.71
  445.4 9.6 %convolution_add_fusion.7 = f32[32,65536]{1,0:T(8,128)} fusion(f32[32,65536]{1,0:T(8,128)} %get-tuple-element.287, pred[]{:T(512)S(6)} %compare.7, f32[1,8,512,128]{3,2,1,0:T(8,128)S(1)} %fusion.71, s32[8]{0:T(128)S(1)} %fusion.72), kind=kOutput, calls=%fused_computation.21.clone.1 | convolution fusion | flops 205521152 | bytes 18874400 | tf_op jit(solution)/shard_map/while/body/eval_jaxpr/dot_general | solution.py:97
  455.0 7.4 reshape.98
  463.8 1.7 convolution_bitcast_fusion
  465.5 1.5 convolution_add_fusion.2
  467.1 175.9 %reduce-scatter.5.cloned.1.call-done = f32[1024,128]{1,0:T(8,128)} async-done(((f32[16384,128]{1,0:T(8,128)}), f32[1024,128]{1,0:T(8,128)}) %reduce-scatter.5.cloned.1.call-update) | async-done | bytes 524304 | tf_op jit(solution)/shard_map/reduce_scatter | solution.py:110
  643.0 2.8 convolution_bitcast_fusion.1
  645.8 2.5 fusion.33
  648.3 244.7 %all-reduce.3.cloned.1.call-done = (f32[128,128]{0,1:T(8,128)}, f32[128,128]{0,1:T(8,128)}) async-done(((f32[128,128]{0,1:T(8,128)}, f32[128,128]{0,1:T(8,128)}), (f32[128,128]{0,1:T(8,128)}, f32[128,128]{0,1:T(8,128)})) %all-reduce.3.cloned.1.call-update) | async-done | bytes 131088 | tf_op jit(solution)/shard_map/psum | solution.py:120
  893.0 1.6 copy.22
  894.6 1.6 copy.23
  (50 shorter events, 4.7 us)
Async XLA Ops:
  7.2 187.9 %copy-start = (f32[128,128]{1,0:T(8,128)S(1)}, f32[128,128]{1,0:T(8,128)}, u32[]{:S(2)}) copy-start(f32[128,128]{1,0:T(8,128)} %param.20) | copy-start | bytes 196612
  7.2 187.9 %all-gather.3.cloned.1.call-start = ((), (), s32[]{:S(2)}) async-start(), calls=%async_computation.2 | async-start | bytes 8912896 | tf_op jit(solution)/shard_map/all_gather | solution.py:38
  7.9 354.7 %reduce-scatter.3.cloned.1.call-start = ((), (), s32[]{:S(2)}) async-start(), calls=%async_computation.3 | async-start | bytes 8912896 | tf_op jit(solution)/shard_map/reduce_scatter | solution.py:68
  251.1 111.4 %copy-start.3 = (f32[1024,128]{1,0:T(8,128)S(1)}, f32[1024,128]{1,0:T(8,128)}, u32[]{:S(2)}) copy-start(f32[1024,128]{1,0:T(8,128)} %param.15) | copy-start | bytes 1572868
  251.1 111.4 %copy-start.5 = (f32[1024,128]{1,0:T(8,128)S(1)}, f32[1024,128]{1,0:T(8,128)}, u32[]{:S(2)}) copy-start(f32[1024,128]{1,0:T(8,128)} %param.25) | copy-start | bytes 1572868
  251.1 111.4 %copy-start.7 = (f32[128,128]{1,0:T(8,128)S(1)}, f32[128,128]{1,0:T(8,128)}, u32[]{:S(2)}) copy-start(f32[128,128]{1,0:T(8,128)} %param.19) | copy-start | bytes 196612
  251.1 111.4 %copy-start.8 = (f32[1024]{0:T(1024)S(1)}, f32[1024]{0:T(1024)}, u32[]{:S(2)}) copy-start(f32[1024]{0:T(1024)} %param.17) | copy-start | bytes 12292
  251.2 174.0 %all-gather.5.cloned.1.call-start = ((), (), s32[]{:S(2)}) async-start(), calls=%async_computation.4 | async-start | bytes 4456448 | tf_op jit(solution)/shard_map/all_gather | solution.py:89
  365.5 277.5 %reduce-scatter.5.cloned.1.call-start = ((), (), s32[]{:S(2)}) async-start(), calls=%async_computation.5 | async-start | bytes 8912896 | tf_op jit(solution)/shard_map/reduce_scatter | solution.py:110
  462.4 1.0 copy-start.4
  462.4 1.2 copy-start.6
  462.4 1.4 copy-start.9
  462.4 180.5 %copy-start.1 = (f32[1024,128]{1,0:T(8,128)S(1)}, f32[1024,128]{1,0:T(8,128)}, u32[]{:S(2)}) copy-start(f32[1024,128]{1,0:T(8,128)} %param.16) | copy-start | bytes 1572868
  462.4 180.5 %copy-start.2 = (f32[1024]{0:T(1024)S(1)}, f32[1024]{0:T(1024)}, u32[]{:S(2)}) copy-start(f32[1024]{0:T(1024)} %param.18) | copy-start | bytes 12292
  462.5 430.6 %all-reduce.3.cloned.1.call-start = ((), (), s32[]{:S(2)}) async-start(), calls=%async_computation.6 | async-start | bytes 262144 | tf_op jit(solution)/shard_map/psum | solution.py:120
Sparse Core Ops, SparseCore 0:
  9.8 185.2 all-gather.2
  251.3 111.2 reduce-scatter.2
  365.9 59.2 all-gather.4
  462.6 180.3 reduce-scatter.4
  649.0 244.0 all-reduce.2
where the time goes:
time: 904 us; the launch traced here: 903 us
  waiting for transfers between devices  726 us (80%)
  matrix products  78.1 us (9%)
  local copies, waits for them, and re-layouts  44 us (5%)
  blocking collectives  37 us (4%)
  between operations  14.6 us (2%)
    psum x1, waiting for transfers between devices, body(): grad_msg, grad_self = lax.psum((local_msg, local_self), ('cg', 'vg'))  245 us
    reduce_scatter x1, waiting for transfers between devices, body(): lax.psum_scatter(backward_sum.reshape(col_blocks * TB, H), 'cg', scatter_...  176 us
    all_gather x1, waiting for transfers between devices, body(): lax.all_gather(var_embed, 'cg', axis=0, tiled=True)  147 us
    reduce_scatter x1, waiting for transfers between devices, body(): lax.psum_scatter(forward_sum.reshape(row_blocks * TB, H), 'vg', scatter_d...  110 us
    all_gather x1, waiting for transfers between devices, body(): lax.all_gather(grad_messages, 'vg', axis=0, tiled=True)  47.1 us
    all_gather x1, blocking collectives, body(): lax.all_gather(col_coef, 'cg', axis=0, tiled=True)  37 us
    dot_general x1, matrix products, body(): jnp.dot(gathered, msg_weight, precision=highest, preferred_element_type=j...  18.7 us
  transfers between devices with their start and end apart: 5, of which 5 were waited for; matrix products, arithmetic and copies ran while one was open for 2% of the time, Pallas kernels for 0%

commit v1 on v0

--- a/solution.py
+++ b/solution.py
@@ -117,7 +117,7 @@
     local_msg = jnp.dot(
         var_embed.T, grad_lin, precision=highest, preferred_element_type=jnp.float32
     )
-    grad_msg, grad_self = lax.psum((local_msg, local_self), ("cg", "vg"))
+    grad_msg, grad_self = lax.psum(lax.psum((local_msg, local_self), "vg"), "cg")
     return (con_update, grad_con, grad_var, grad_msg, grad_self)
 
 

time: 904 us -> 940 us (1.040)
  waiting for transfers between devices: 726 us -> 761 us
    psum x1 -> x2, waiting for transfers between devices: 245 us -> 279 us  [the longest x1 142 us: body(): lax.psum((local_msg, local_self), 'vg')]
  transfers between devices with their start and end apart: 5 -> 6, of which waited for: 5 -> 6; matrix products, arithmetic and copies ran while one was open for 2% -> 2% of each run, Pallas kernels for 0% -> 0%
where the time goes in v1:
time: 940 us; the launch traced here: 939 us
  waiting for transfers between devices  761 us (81%)
  matrix products  78.2 us (8%)
  local copies, waits for them, and re-layouts  43.9 us (5%)
  blocking collectives  37 us (4%)
  between operations  14.9 us (2%)
    reduce_scatter x1, waiting for transfers between devices, body(): lax.psum_scatter(backward_sum.reshape(col_blocks * TB, H), 'cg', scatter_...  177 us
    all_gather x1, waiting for transfers between devices, body(): lax.all_gather(var_embed, 'cg', axis=0, tiled=True)  147 us
    psum x1, waiting for transfers between devices, body(): lax.psum((local_msg, local_self), 'vg')  142 us
    psum x1, waiting for transfers between devices, body(): lax.psum(lax.psum((local_msg, local_self), 'vg'), 'cg')  137 us
    reduce_scatter x1, waiting for transfers between devices, body(): lax.psum_scatter(forward_sum.reshape(row_blocks * TB, H), 'vg', scatter_d...  110 us
    all_gather x1, waiting for transfers between devices, body(): lax.all_gather(grad_messages, 'vg', axis=0, tiled=True)  47.2 us
    all_gather x1, blocking collectives, body(): lax.all_gather(col_coef, 'cg', axis=0, tiled=True)  37 us
  transfers between devices with their start and end apart: 6, of which 6 were waited for; matrix products, arithmetic and copies ran while one was open for 2% of the time, Pallas kernels for 0%

profile of v1, /device:TPU:2, one launch (start us, length us, event | category | flops | bytes accessed | tf_op | source)
XLA Modules:
  0.0 938.7 jit_solution(16846181656173935909)
XLA Ops:
  11.3 37.0 %all_gather.10 = f32[16384]{0:T(1024)S(1)} all-gather(f32[1024]{0:T(1024)} %param.18), channel_id=1, replica_groups=mesh['cg'=16,'vg'=16] {'cg'}, dimensions={0}, use_global_device_ids=true | all-gather | bytes 69632 | tf_op jit(solution)/shard_map/all_gather | solution.py:39
  48.3 146.8 %all-gather.3.cloned.1.call-done = f32[16384,128]{1,0:T(8,128)} async-done(((f32[1024,128]{1,0:T(8,128)}), f32[16384,128]{1,0:T(8,128)}) %all-gather.3.cloned.1.call-update) | async-done | bytes 8388624 | tf_op jit(solution)/shard_map/all_gather | solution.py:38
  195.1 18.7 %fusion.30 = bf16[16384,128]{1,0:T(8,128)(2,1)} fusion(f32[16384,128]{1,0:T(8,128)} %all-gather.3.cloned.1.call-done, f32[128,128]{1,0:T(8,128)S(1)} %copy-done, f32[16384]{0:T(1024)S(1)} %all_gather.10), kind=kOutput, calls=%fused_computation.39 | convolution fusion | flops 3225419776 | bytes 12713984 | tf_op jit(solution)/shard_map/dot_general | solution.py:42
  213.7 30.1 %while.22 = (s32[]{:T(128)}, f32[32,65536]{1,0:T(8,128)}, s32[2,8]{1,0:T(2,128)S(1)}, bf16[2,8,512,512]{3,2,1,0:T(8,128)(2,1)}, s32[2,8]{1,0:T(2,128)S(1)}, /*in...) while((s32[]{:T(128)}, f32[32,65536]{1,0:T(8,128)}, s32[2,8]{1,0:T(2,128)S(1)}, ...), condition=%wide.region_1.2_spmd.clone, body=%wide.region_0.1_spmd.clone.sunk | while | flops 742393088 | bytes 28316484 | solution.py:63
  213.8 2.9 gather_fusion
  216.7 3.4 fusion.65
  220.2 7.6 convolution_add_fusion.6
  227.8 2.9 gather_fusion
  230.7 3.4 fusion.65
  234.2 9.7 %convolution_add_fusion.6 = f32[32,65536]{1,0:T(8,128)} fusion(f32[32,65536]{1,0:T(8,128)} %get-tuple-element.265, pred[]{:T(512)S(6)} %compare.6, f32[1,8,512,128]{3,2,1,0:T(8,128)S(1)} %fusion.65, s32[8]{0:T(128)S(1)} %fusion.66), kind=kOutput, calls=%fused_computation.4.clone.1 | convolution fusion | flops 205521152 | bytes 18874400 | tf_op jit(solution)/shard_map/while/body/eval_jaxpr/dot_general | solution.py:55
  243.9 7.3 reshape.96
  252.2 110.4 %reduce-scatter.3.cloned.1.call-done = f32[1024,128]{1,0:T(8,128)} async-done(((f32[16384,128]{1,0:T(8,128)}), f32[1024,128]{1,0:T(8,128)}) %reduce-scatter.3.cloned.1.call-update) | async-done | bytes 524304 | tf_op jit(solution)/shard_map/reduce_scatter | solution.py:68
  362.6 2.8 multiply_convert_fusion
  365.7 12.3 %copy.20 = bf16[1,1,16,512,512]{3,4,2,1,0:T(8,128)(2,1)} copy(bf16[1,1,16,512,512]{4,3,2,1,0:T(8,128)(2,1)} %bitcast.88) | data formatting | bytes 16777216 | tf_op args[9]
  378.0 47.2 %all-gather.5.cloned.1.call-done = bf16[16384,128]{1,0:T(8,128)(2,1)} async-done(((bf16[1024,128]{1,0:T(8,128)(2,1)}), bf16[16384,128]{1,0:T(8,128)(2,1)}) %all-gather.5.cloned.1.call-update) | async-done | bytes 4194320 | tf_op jit(solution)/shard_map/all_gather | solution.py:89
  425.2 30.0 %while.23 = (s32[]{:T(128)}, f32[32,65536]{1,0:T(8,128)}, s32[2,8]{1,0:T(2,128)S(1)}, bf16[2,8,512,512]{2,3,1,0:T(8,128)(2,1)}, s32[2,8]{1,0:T(2,128)S(1)}, /*in...) while((s32[]{:T(128)}, f32[32,65536]{1,0:T(8,128)}, s32[2,8]{1,0:T(2,128)S(1)}, ...), condition=%wide.region_4.5_spmd.clone, body=%wide.region_3.4_spmd.clone.sunk | while | flops 742393088 | bytes 28316484 | solution.py:105
  425.2 2.9 gather_fusion.1
  428.2 3.4 fusion.71
  431.6 7.5 convolution_add_fusion.7
  439.1 2.9 gather_fusion.1
  442.1 3.4 fusion.71
  445.5 9.6 %convolution_add_fusion.7 = f32[32,65536]{1,0:T(8,128)} fusion(f32[32,65536]{1,0:T(8,128)} %get-tuple-element.289, pred[]{:T(512)S(6)} %compare.7, f32[1,8,512,128]{3,2,1,0:T(8,128)S(1)} %fusion.71, s32[8]{0:T(128)S(1)} %fusion.72), kind=kOutput, calls=%fused_computation.21.clone.1 | convolution fusion | flops 205521152 | bytes 18874400 | tf_op jit(solution)/shard_map/while/body/eval_jaxpr/dot_general | solution.py:97
  455.2 7.4 reshape.98
  463.9 1.7 convolution_bitcast_fusion
  465.7 177.4 %reduce-scatter.5.cloned.1.call-done = f32[1024,128]{1,0:T(8,128)} async-done(((f32[16384,128]{1,0:T(8,128)}), f32[1024,128]{1,0:T(8,128)}) %reduce-scatter.5.cloned.1.call-update) | async-done | bytes 524304 | tf_op jit(solution)/shard_map/reduce_scatter | solution.py:110
  643.1 2.8 convolution_bitcast_fusion.1
  646.0 1.5 convolution_add_fusion.2
  647.5 142.1 %all-reduce.5.cloned.1.call-done = (f32[128,128]{0,1:T(8,128)}, f32[128,128]{0,1:T(8,128)}) async-done(((f32[128,128]{0,1:T(8,128)}, f32[128,128]{0,1:T(8,128)}), (f32[128,128]{0,1:T(8,128)}, f32[128,128]{0,1:T(8,128)})) %all-reduce.5.cloned.1.call-update) | async-done | bytes 131088 | tf_op jit(solution)/shard_map/psum | solution.py:120
  789.7 2.5 fusion.33
  792.2 136.6 %all-reduce.7.cloned.1.call-done = (f32[128,128]{0,1:T(8,128)}, f32[128,128]{0,1:T(8,128)}) async-done(((f32[128,128]{0,1:T(8,128)}, f32[128,128]{0,1:T(8,128)}), (f32[128,128]{0,1:T(8,128)}, f32[128,128]{0,1:T(8,128)})) %all-reduce.7.cloned.1.call-update) | async-done | bytes 131088 | tf_op jit(solution)/shard_map/psum | solution.py:120
  928.7 1.6 copy.22
  930.3 1.6 copy.23
  (53 shorter events, 6.0 us)
Async XLA Ops:
  7.2 187.9 %copy-start = (f32[128,128]{1,0:T(8,128)S(1)}, f32[128,128]{1,0:T(8,128)}, u32[]{:S(2)}) copy-start(f32[128,128]{1,0:T(8,128)} %param.20) | copy-start | bytes 196612
  7.2 187.9 %all-gather.3.cloned.1.call-start = ((), (), s32[]{:S(2)}) async-start(), calls=%async_computation.2 | async-start | bytes 8912896 | tf_op jit(solution)/shard_map/all_gather | solution.py:38
  7.9 354.7 %reduce-scatter.3.cloned.1.call-start = ((), (), s32[]{:S(2)}) async-start(), calls=%async_computation.3 | async-start | bytes 8912896 | tf_op jit(solution)/shard_map/reduce_scatter | solution.py:68
  251.2 111.4 %copy-start.3 = (f32[1024,128]{1,0:T(8,128)S(1)}, f32[1024,128]{1,0:T(8,128)}, u32[]{:S(2)}) copy-start(f32[1024,128]{1,0:T(8,128)} %param.15) | copy-start | bytes 1572868
  251.2 111.4 %copy-start.5 = (f32[1024,128]{1,0:T(8,128)S(1)}, f32[1024,128]{1,0:T(8,128)}, u32[]{:S(2)}) copy-start(f32[1024,128]{1,0:T(8,128)} %param.25) | copy-start | bytes 1572868
  251.2 111.4 %copy-start.7 = (f32[128,128]{1,0:T(8,128)S(1)}, f32[128,128]{1,0:T(8,128)}, u32[]{:S(2)}) copy-start(f32[128,128]{1,0:T(8,128)} %param.19) | copy-start | bytes 196612
  251.2 111.4 %copy-start.8 = (f32[1024]{0:T(1024)S(1)}, f32[1024]{0:T(1024)}, u32[]{:S(2)}) copy-start(f32[1024]{0:T(1024)} %param.17) | copy-start | bytes 12292
  251.2 173.9 %all-gather.5.cloned.1.call-start = ((), (), s32[]{:S(2)}) async-start(), calls=%async_computation.4 | async-start | bytes 4456448 | tf_op jit(solution)/shard_map/all_gather | solution.py:89
  365.5 277.6 %reduce-scatter.5.cloned.1.call-start = ((), (), s32[]{:S(2)}) async-start(), calls=%async_computation.5 | async-start | bytes 8912896 | tf_op jit(solution)/shard_map/reduce_scatter | solution.py:110
  462.6 1.0 copy-start.4
  462.6 1.2 copy-start.6
  462.6 1.4 copy-start.9
  462.6 180.5 %copy-start.1 = (f32[1024,128]{1,0:T(8,128)S(1)}, f32[1024,128]{1,0:T(8,128)}, u32[]{:S(2)}) copy-start(f32[1024,128]{1,0:T(8,128)} %param.16) | copy-start | bytes 1572868
  462.6 180.5 %copy-start.2 = (f32[1024]{0:T(1024)S(1)}, f32[1024]{0:T(1024)}, u32[]{:S(2)}) copy-start(f32[1024]{0:T(1024)} %param.18) | copy-start | bytes 12292
  462.6 327.1 %all-reduce.5.cloned.1.call-start = ((), (), s32[]{:S(2)}) async-start(), calls=%async_computation.6 | async-start | bytes 262144 | tf_op jit(solution)/shard_map/psum | solution.py:120
  646.0 282.8 %all-reduce.7.cloned.1.call-start = ((), (), s32[]{:S(2)}) async-start(), calls=%async_computation.7 | async-start | bytes 262144 | tf_op jit(solution)/shard_map/psum | solution.py:120
Sparse Core Ops, SparseCore 0:
  9.8 185.2 all-gather.2
  251.4 111.1 reduce-scatter.2
  365.9 59.2 all-gather.4
  462.7 180.3 reduce-scatter.4
  646.2 143.4 all-reduce.4
  792.4 136.3 all-reduce.6
